TPU v7x, 256 devices: a whole 4x4x8 slice. The times are simulated.
256 devices in a mesh: dp: 8 (over z_lo, x), expert: 32 (over y, z_hi, core).
Axes of the slice: x: 4, y: 4, z: 8 (z_hi: 4, z_lo: 2; z = z_hi * 2 + z_lo), core: 2. Of those that a mesh axis runs over, the one named last changes fastest.
Arguments:
- tokens: bfloat16 [4096, 7168], P('expert', 'dp'), may hold values from -6 to 6
- cotangent: bfloat16 [4096, 7168], P('expert', 'dp'), may hold values from -6 to 6
- routes: int32 [4096, 4], P('expert'), may hold values from 0 to 31, all different within a row; in each aligned block of 128 rows (0 to 127, 128 to 255, ...) at most 24 rows name the same one
- combine_weights: float32 [4096, 4], P('expert'), may hold values from 0.2 to 1
- gate_weight: bfloat16 [32, 7168, 1024], P('expert', 'dp'), may hold values from -0.0625 to 0.0625
- up_weight: bfloat16 [32, 7168, 1024], P('expert', 'dp'), may hold values from -0.0625 to 0.0625
- down_weight: bfloat16 [32, 1024, 7168], P('expert', None, 'dp'), may hold values from -0.1875 to 0.1875
Outputs:
- grad_tokens: bfloat16 [4096, 7168], P('expert', 'dp')
- grad_gate: bfloat16 [32, 7168, 1024], P('expert', 'dp')
- grad_up: bfloat16 [32, 7168, 1024], P('expert', 'dp')
- grad_down: bfloat16 [32, 1024, 7168], P('expert', None, 'dp')
Inputs may be any that keep to these rules, and one draw needn't show every extreme that they name: `routes`: each row names 4 different experts. Within each aligned block of 128 tokens no expert is named by more than 24 tokens, and in every draw some block has an expert named by exactly 24 tokens.
All inputs are finite; a program needn't handle non-finite values.
Results may differ from a plain program's by a relative error of at most 0.029.
Values may be sent and summed in bfloat16 or wider, within the bound.
No kernel may reach another device: no remote copies, remote signals or barrier semaphores. Data moves between devices by JAX's collectives and lax.ppermute only.
A program may use at most 64 MiB of HBM per device.

v0:
```python
import jax
import jax.numpy as jnp
from jax import lax
from jax.sharding import PartitionSpec as P


def contract(left, right, left_dim, right_dim):
    return lax.dot_general(
        left, right, (((left_dim,), (right_dim,)), ((), ())), preferred_element_type=jnp.float32
    )


def local(tokens, cotangent, routes, combine_weights, gate_weight, up_weight, down_weight):
    experts = lax.axis_size("expert")
    tok_count = routes.shape[0]
    top_count = routes.shape[1]
    width = tokens.shape[1]
    capacity = 3 * tok_count * top_count // (2 * experts)
    flat_routes = routes.reshape(-1)
    onehot = (flat_routes[:, None] == jnp.arange(experts, dtype=jnp.int32)[None, :]).astype(
        jnp.int32
    )
    slot_rank = jnp.sum((jnp.cumsum(onehot, axis=0) - onehot) * onehot, axis=1)
    slots = flat_routes * capacity + slot_rank
    x_pairs = jnp.repeat(tokens, top_count, axis=0)
    scaled = (combine_weights[:, :, None] * cotangent[:, None, :].astype(jnp.float32)).astype(
        jnp.bfloat16
    )
    scaled = scaled.reshape(tok_count * top_count, width)
    empty = jnp.zeros((experts * capacity, width), jnp.bfloat16)
    send_x = empty.at[slots].set(x_pairs).reshape(experts, capacity, width)
    send_s = empty.at[slots].set(scaled).reshape(experts, capacity, width)
    weight_g = gate_weight[0]
    weight_u = up_weight[0]
    weight_d = down_weight[0]
    recv_x, recv_s = (
        lax.all_to_all(send_x, "expert", split_axis=0, concat_axis=0, tiled=True),
        lax.all_to_all(send_s, "expert", split_axis=0, concat_axis=0, tiled=True),
    )
    gate_part = jnp.dot(
        recv_x.reshape(-1, width), weight_g, preferred_element_type=jnp.float32
    ).astype(jnp.bfloat16)
    up_part = jnp.dot(
        recv_x.reshape(-1, width), weight_u, preferred_element_type=jnp.float32
    ).astype(jnp.bfloat16)
    rows_x = recv_x.reshape(-1, width)
    rows_s = recv_s.reshape(-1, width)
    back_part = contract(rows_s, weight_d, 1, 1).astype(jnp.bfloat16)
    gate_share, upper_share = (
        lax.psum_scatter(gate_part, "dp", scatter_dimension=1, tiled=True).astype(jnp.float32),
        lax.psum_scatter(up_part, "dp", scatter_dimension=1, tiled=True).astype(jnp.float32),
    )
    activation = jax.nn.silu(gate_share)
    hidden_share = (activation * upper_share).astype(jnp.bfloat16)
    hidden = lax.all_gather(hidden_share, "dp", axis=1, tiled=True)
    dhidden = lax.psum_scatter(back_part, "dp", scatter_dimension=1, tiled=True).astype(jnp.float32)
    sigmoid_g = jax.nn.sigmoid(gate_share)
    slope = sigmoid_g * (1.0 + gate_share * (1.0 - sigmoid_g))
    gate_grad_share = (dhidden * upper_share * slope).astype(jnp.bfloat16)
    up_grad_share = (dhidden * activation).astype(jnp.bfloat16)
    pre_gate, pre_up = (
        lax.all_gather(gate_grad_share, "dp", axis=1, tiled=True),
        lax.all_gather(up_grad_share, "dp", axis=1, tiled=True),
    )
    back_rows = (contract(pre_gate, weight_g, 1, 1) + contract(pre_up, weight_u, 1, 1)).astype(
        jnp.bfloat16
    )
    returned = lax.all_to_all(
        back_rows.reshape(experts, capacity, width),
        "expert",
        split_axis=0,
        concat_axis=0,
        tiled=True,
    )
    grad_down = contract(hidden, rows_s, 0, 0).astype(jnp.bfloat16)[None]
    grad_gate = contract(rows_x, pre_gate, 0, 0).astype(jnp.bfloat16)[None]
    grad_up = contract(rows_x, pre_up, 0, 0).astype(jnp.bfloat16)[None]
    picked = returned.reshape(experts * capacity, width)[slots]
    grad_tokens = jnp.sum(
        picked.reshape(tok_count, top_count, width).astype(jnp.float32), axis=1
    ).astype(jnp.bfloat16)
    return (grad_tokens, grad_gate, grad_up, grad_down)


def solution(mesh):
    placed = (
        P("expert", "dp"),
        P("expert", "dp"),
        P("expert", None),
        P("expert", None),
        P("expert", "dp", None),
        P("expert", "dp", None),
        P("expert", None, "dp"),
    )
    return jax.shard_map(
        local,
        mesh=mesh,
        in_specs=placed,
        out_specs=(
            P("expert", "dp"),
            P("expert", "dp", None),
            P("expert", "dp", None),
            P("expert", None, "dp"),
        ),
        check_vma=False,
    )
```

profile of v0, /device:TPU:1, one launch (start us, length us, event | category | flops | bytes accessed | tf_op | source)
XLA Modules:
  0.0 386.5 jit_solution(345836730867990617)
XLA Ops:
  7.2 0.0 copy-start
  7.2 0.0 reduce-scatter.12.cloned.1.call-start
  7.2 0.9 copy.17
  8.1 0.1 eq.29
  8.2 0.1 eq.25
  8.4 0.7 broadcast_multiply_fusion
  9.1 1.2 reduce-window.6
  10.2 0.2 slice_reduce_fusion
  10.5 0.1 copy.16
  10.6 0.1 mul.61
  10.7 1.2 broadcast_in_dim.22
  11.9 1.1 reshape.116
  13.0 0.1 fusion.37
  13.1 3.5 scatter_custom_fusion.1
  16.7 0.0 copy-start.7
  16.7 49.8 %all_to_all.15 = bf16[32,24,896]{2,1,0:T(8,128)(2,1)S(1)} all-to-all(bf16[32,24,896]{2,1,0:T(8,128)(2,1)S(1)} %bitcast.76), channel_id=1, replica_groups=mesh['dp'=8,'expert'=32] {'expert'}, dimensions={0} | all-to-all | bytes 2752512 | tf_op jit(solution)/shard_map/all_to_all | solution.py:37
  66.5 1.2 copy-done.1
  67.7 1.8 fusion.13
  69.5 1.6 copy.23
  71.0 0.0 reduce-scatter.12.cloned.1.call-update
  71.1 0.0 reduce-scatter.14.cloned.1.call-start
  71.1 3.1 fusion.16
  74.3 1.6 copy.25
  75.9 0.0 reduce-scatter.14.cloned.1.call-update
  75.9 0.0 reduce-scatter.10.cloned.1.call-start
  75.9 0.9 copy-done.4
  76.8 1.5 mul.65
  78.3 2.8 mul.66
  81.1 0.0 copy-done.5
  81.1 0.1 copy.20
  81.2 0.1 mul.63
  81.3 3.9 %scatter_custom_fusion = bf16[768,896]{1,0:T(8,128)(2,1)S(1)} fusion(s32[512]{0:T(512)S(1)} %bitcast.88, f32[512,896]{1,0:T(8,128)} %mul.66, f32[512]{0:T(512)S(1)} %mul.63, bf16[]{:T(256)} %constant.5.clone.1), kind=kCustom, calls=%fused_computation.21 | custom fusion | flops 917504 | bytes 3213314 | tf_op jit(solution)/shard_map/scatter | solution.py:32
  85.3 0.0 copy-start.6
  85.3 48.7 %all_to_all.16 = bf16[32,24,896]{2,1,0:T(8,128)(2,1)S(1)} all-to-all(bf16[32,24,896]{2,1,0:T(8,128)(2,1)S(1)} %bitcast.75), channel_id=1, replica_groups=mesh['dp'=8,'expert'=32] {'expert'}, dimensions={0} | all-to-all | bytes 2752512 | tf_op jit(solution)/shard_map/all_to_all | solution.py:38
  133.9 1.1 copy-done.3
  135.1 1.8 fusion.10
  136.9 1.6 copy.21
  138.5 0.0 reduce-scatter.10.cloned.1.call-update
  138.5 0.0 all-gather.4.cloned.1.call-start
  138.6 0.0 reduce-scatter.12.cloned.1.call-done
  138.6 1.1 copy.24
  139.7 22.9 %reduce-scatter.14.cloned.1.call-done = bf16[128,768]{1,0:T(8,128)(2,1)} async-done(((bf16[1024,768]{1,0:T(8,128)(2,1)}), bf16[128,768]{1,0:T(8,128)(2,1)}) %reduce-scatter.14.cloned.1.call-update) | async-done | bytes 196624
  162.6 1.1 copy.26
  163.7 44.3 %reduce-scatter.10.cloned.1.call-done = bf16[128,768]{1,0:T(8,128)(2,1)} async-done(((bf16[1024,768]{1,0:T(8,128)(2,1)}), bf16[128,768]{1,0:T(8,128)(2,1)}) %reduce-scatter.10.cloned.1.call-update) | async-done | bytes 196624
  208.0 1.1 copy.22
  209.1 1.0 fusion.29
  210.1 0.0 all-gather.4.cloned.1.call-update
  210.2 0.0 all-gather.6.cloned.1.call-start
  210.2 0.5 all-gather.6.cloned.1.call-update
  210.8 0.0 all-gather.8.cloned.1.call-start
  210.8 0.5 all-gather.8.cloned.1.call-update
  211.3 42.8 %all-gather.4.cloned.1.call-done = bf16[768,1024]{1,0:T(8,128)(2,1)} async-done(((bf16[768,128]{1,0:T(8,128)(2,1)}), bf16[768,1024]{1,0:T(8,128)(2,1)}) %all-gather.4.cloned.1.call-update) | async-done | bytes 1572880 | tf_op jit(solution)/shard_map/all_gather | solution.py:62
  254.1 4.8 %fusion = f32[768,896]{1,0:T(8,128)} fusion(bf16[768,1024]{1,0:T(8,128)(2,1)} %all-gather.4.cloned.1.call-done, bf16[1,896,1024]{2,1,0:T(8,128)(2,1)S(1)} %copy-done), kind=kOutput, calls=%fused_computation.4 | convolution fusion | flops 1409286144 | bytes 6160384 | tf_op jit(solution)/shard_map/dot_general | solution.py:8
  258.9 42.3 %all-gather.6.cloned.1.call-done = bf16[768,1024]{1,0:T(8,128)(2,1)} async-done(((bf16[768,128]{1,0:T(8,128)(2,1)}), bf16[768,1024]{1,0:T(8,128)(2,1)}) %all-gather.6.cloned.1.call-update) | async-done | bytes 1572880 | tf_op jit(solution)/shard_map/all_gather | solution.py:63
  301.3 5.7 %add_convert_fusion = bf16[768,896]{1,0:T(8,128)(2,1)} fusion(f32[768,896]{1,0:T(8,128)} %fusion, bf16[768,1024]{1,0:T(8,128)(2,1)} %all-gather.6.cloned.1.call-done, bf16[1,896,1024]{2,1,0:T(8,128)(2,1)} %param.12), kind=kOutput, calls=%fused_computation.3 | convolution fusion | flops 1410662400 | bytes 7536640 | tf_op jit(solution)/shard_map/dot_general | solution.py:8
  307.0 14.1 %all-to-all-start.2 = ((bf16[32,24,896]{2,1,0:T(8,128)(2,1)}), bf16[32,24,896]{2,1,0:T(8,128)(2,1)S(1)}, u32[]{:S(2)}, u32[]{:S(2)}) async-start(bf16[32,24,896]{2,1,0:T(8,128)(2,1)} %bitcast.83), calls=%async_computation.2 | async-start | bytes 2752512 | tf_op jit(solution)/shard_map/all_to_all | solution.py:68
  321.1 4.8 %convert_bitcast_fusion.1 = bf16[1,896,1024]{2,1,0:T(8,128)(2,1)} fusion(bf16[768,896]{1,0:T(8,128)(2,1)} %bitcast.79, bf16[768,1024]{1,0:T(8,128)(2,1)} %all-gather.6.cloned.1.call-done), kind=kOutput, calls=%fused_computation.15 | convolution fusion | flops 1410203648 | bytes 4784128 | tf_op jit(solution)/shard_map/dot_general | solution.py:8
  325.9 2.9 convert_bitcast_fusion.2
  328.8 39.6 %all-gather.8.cloned.1.call-done = bf16[768,1024]{1,0:T(8,128)(2,1)} async-done(((bf16[768,128]{1,0:T(8,128)(2,1)}), bf16[768,1024]{1,0:T(8,128)(2,1)}) %all-gather.8.cloned.1.call-update) | async-done | bytes 1572880 | tf_op jit(solution)/shard_map/all_gather | solution.py:55
  368.4 4.9 %convert_bitcast_fusion = bf16[1,1024,896]{2,1,0:T(8,128)(2,1)} fusion(bf16[768,1024]{1,0:T(8,128)(2,1)} %all-gather.8.cloned.1.call-done, bf16[768,896]{1,0:T(8,128)(2,1)} %bitcast.82), kind=kOutput, calls=%fused_computation.14 | convolution fusion | flops 1410203648 | bytes 4784128 | tf_op jit(solution)/shard_map/dot_general | solution.py:8
  373.3 0.0 all-to-all-done.2
  373.3 2.7 gather_fusion
  376.0 1.8 reshape.95
  377.8 1.9 reduce_sum.25
  (16 shorter events, 0.1 us)
Async XLA Ops:
  7.2 64.0 %copy-start = (bf16[1,896,1024]{2,1,0:T(8,128)(2,1)S(1)}, bf16[1,896,1024]{2,1,0:T(8,128)(2,1)}, u32[]{:S(2)}) copy-start(bf16[1,896,1024]{2,1,0:T(8,128)(2,1)} %param.11) | copy-start | bytes 5505028
  7.2 131.4 %reduce-scatter.12.cloned.1.call-start = ((), (), s32[]{:S(2)}) async-start(), calls=%async_computation.10 | async-start | bytes 1769472
  16.7 51.0 %copy-start.7 = (bf16[1,896,1024]{2,1,0:T(8,128)(2,1)S(1)}, bf16[1,896,1024]{2,1,0:T(8,128)(2,1)}, u32[]{:S(2)}) copy-start(bf16[1,896,1024]{2,1,0:T(8,128)(2,1)} %param.12) | copy-start | bytes 5505028
  66.5 1.2 copy-start.1
  71.1 91.6 %reduce-scatter.14.cloned.1.call-start = ((), (), s32[]{:S(2)}) async-start(), calls=%async_computation.11 | async-start | bytes 1769472
  75.9 0.9 copy-start.4
  75.9 132.1 %reduce-scatter.10.cloned.1.call-start = ((), (), s32[]{:S(2)}) async-start(), calls=%async_computation.9 | async-start | bytes 1769472
  78.3 2.9 copy-start.5
  85.3 49.8 %copy-start.6 = (bf16[1,1024,896]{2,1,0:T(8,128)(2,1)S(1)}, bf16[1,1024,896]{2,1,0:T(8,128)(2,1)}, u32[]{:S(2)}) copy-start(bf16[1,1024,896]{2,1,0:T(8,128)(2,1)} %param.13) | copy-start | bytes 5505028
  133.9 1.1 copy-start.3
  138.5 115.6 %all-gather.4.cloned.1.call-start = ((), (), s32[]{:S(2)}) async-start(), calls=%async_computation.6 | async-start | bytes 1769472 | tf_op jit(solution)/shard_map/all_gather | solution.py:62
  210.2 91.1 %all-gather.6.cloned.1.call-start = ((), (), s32[]{:S(2)}) async-start(), calls=%async_computation.7 | async-start | bytes 1769472 | tf_op jit(solution)/shard_map/all_gather | solution.py:63
  210.8 157.6 %all-gather.8.cloned.1.call-start = ((), (), s32[]{:S(2)}) async-start(), calls=%async_computation.8 | async-start | bytes 1769472 | tf_op jit(solution)/shard_map/all_gather | solution.py:55
  307.0 66.3 %all-to-all-start.2 = ((bf16[32,24,896]{2,1,0:T(8,128)(2,1)}), bf16[32,24,896]{2,1,0:T(8,128)(2,1)S(1)}, u32[]{:S(2)}, u32[]{:S(2)}) async-start(bf16[32,24,896]{2,1,0:T(8,128)(2,1)} %bitcast.83), calls=%async_computation.2 | async-start | bytes 2752512 | tf_op jit(solution)/shard_map/all_to_all | solution.py:68
  321.1 4.8 %copy-start.2 = (bf16[32,24,896]{2,1,0:T(8,128)(2,1)S(1)}, bf16[32,24,896]{2,1,0:T(8,128)(2,1)}, u32[]{:S(2)}) copy-start(bf16[32,24,896]{2,1,0:T(8,128)(2,1)} %copy-done.1) | copy-start | bytes 4128772
  321.1 4.8 %copy-start.8 = (bf16[768,1024]{1,0:T(8,128)(2,1)S(1)}, bf16[768,1024]{1,0:T(8,128)(2,1)}, u32[]{:S(2)}) copy-start(bf16[768,1024]{1,0:T(8,128)(2,1)} %all-gather.4.cloned.1.call-done) | copy-start | bytes 4718596
Sparse Core Ops, SparseCore 0:
  71.2 48.9 reduce-scatter.11
  122.7 39.8 reduce-scatter.13
  165.8 42.2 reduce-scatter.9
  210.3 43.8 all-gather.3
  256.3 44.9 all-gather.5
  303.4 64.9 all-gather.7
where the time goes:
time: 387 us
  waiting for transfers between devices  193 us (50%)
  blocking collectives  98.5 us (25%)
  matrix products  29.8 us (8%)
  local copies, waits for them, and re-layouts  27.7 us (7%)
  starting transfers between devices  14.3 us (4%)
  between operations  14.3 us (4%)
  other arithmetic  8.87 us (2%)
    unnamed x9, waiting for transfers between devices  68.4 us
    all_to_all x1, blocking collectives, local(): lax.all_to_all(send_x, 'expert', split_axis=0, concat_axis=0, tiled=True)  49.8 us
    all_to_all x1, blocking collectives, local(): lax.all_to_all(send_s, 'expert', split_axis=0, concat_axis=0, tiled=True)  48.7 us
    all_gather x1, waiting for transfers between devices, local(): lax.all_gather(gate_grad_share, 'dp', axis=1, tiled=True)  42.8 us
    all_gather x1, waiting for transfers between devices, local(): lax.all_gather(up_grad_share, 'dp', axis=1, tiled=True)  42.3 us
    all_gather x1, waiting for transfers between devices, local(): hidden = lax.all_gather(hidden_share, 'dp', axis=1, tiled=True)  39.6 us
    dot_general x6, matrix products, contract(): lax.dot_general(left, right, (((left_dim,), (right_dim,)), ((), ())), pre...  24.9 us
    all_to_all x1, starting transfers between devices, local(): lax.all_to_all(back_rows.reshape(experts, capacity, width), 'expert', spl...  14.1 us
  transfers between devices with their start and end apart: 7, of which 5 were waited for; matrix products, arithmetic and copies ran while one was open for 11% of the time, Pallas kernels for 0%

commit v1 on v0

--- a/solution.py
+++ b/solution.py
@@ -60,7 +60,9 @@
     up_grad_share = (dhidden * activation).astype(jnp.bfloat16)
     pre_gate, pre_up = (
         lax.all_gather(gate_grad_share, "dp", axis=1, tiled=True),
-        lax.all_gather(up_grad_share, "dp", axis=1, tiled=True),
+        jnp.concatenate(
+            lax.all_to_all(jnp.stack([up_grad_share] * lax.axis_size("dp")), "dp", 0, 0), axis=1
+        ),
     )
     back_rows = (contract(pre_gate, weight_g, 1, 1) + contract(pre_up, weight_u, 1, 1)).astype(
         jnp.bfloat16

time: 387 us -> 347 us (0.90)
  waiting for transfers between devices: 193 us -> 147 us
    all_gather x1 -> x0, waiting for transfers between devices: 42.3 us -> none  [local(): lax.all_gather(up_grad_share, 'dp', axis=1, tiled=True)]
    all_gather x1, waiting for transfers between devices: 39.6 us -> 32.8 us  [local(): hidden = lax.all_gather(hidden_share, 'dp', axis=1, tiled=True)]
    unnamed x9 -> x8, waiting for transfers between devices: 68.4 us -> 68 us
    unnamed x26 -> x28, local copies, waits for them, and re-layouts: 12.2 us -> 12.2 us
  transfers between devices with their start and end apart: 7 -> 7, of which waited for: 5 -> 5; matrix products, arithmetic and copies ran while one was open for 11% -> 13% of each run, Pallas kernels for 0% -> 0%
where the time goes in v1:
time: 347 us; the launch traced here: 345 us
  waiting for transfers between devices  147 us (42%)
  blocking collectives  98.5 us (28%)
  matrix products  30.1 us (9%)
  local copies, waits for them, and re-layouts  29 us (8%)
  starting transfers between devices  17.9 us (5%)
  between operations  14 us (4%)
  other arithmetic  8.84 us (3%)
    unnamed x8, waiting for transfers between devices  68 us
    all_to_all x1, blocking collectives, local(): lax.all_to_all(send_x, 'expert', split_axis=0, concat_axis=0, tiled=True)  49.8 us
    all_to_all x1, blocking collectives, local(): lax.all_to_all(send_s, 'expert', split_axis=0, concat_axis=0, tiled=True)  48.7 us
    all_gather x1, waiting for transfers between devices, local(): lax.all_gather(gate_grad_share, 'dp', axis=1, tiled=True)  44.4 us
    all_gather x1, waiting for transfers between devices, local(): hidden = lax.all_gather(hidden_share, 'dp', axis=1, tiled=True)  32.8 us
    dot_general x6, matrix products, contract(): lax.dot_general(left, right, (((left_dim,), (right_dim,)), ((), ())), pre...  25.2 us
    all_to_all x1, starting transfers between devices, local(): lax.all_to_all(back_rows.reshape(experts, capacity, width), 'expert', spl...  13.9 us
    unnamed x28, local copies, waits for them, and re-layouts  12.2 us
  transfers between devices with their start and end apart: 7, of which 5 were waited for; matrix products, arithmetic and copies ran while one was open for 13% of the time, Pallas kernels for 0%

profile of v1, /device:TPU:1, one launch (start us, length us, event | category | flops | bytes accessed | tf_op | source)
XLA Modules:
  0.0 345.4 jit_solution(4102823642528729209)
XLA Ops:
  7.2 0.0 copy-start
  7.2 0.0 reduce-scatter.12.cloned.1.call-start
  7.2 0.9 copy.18
  8.1 0.1 eq.29
  8.2 0.1 eq.25
  8.4 0.7 broadcast_multiply_fusion
  9.1 1.2 reduce-window.6
  10.2 0.2 slice_reduce_fusion
  10.5 0.1 copy.17
  10.6 0.1 mul.61
  10.7 1.2 broadcast_in_dim.22
  11.9 1.1 reshape.126
  13.0 0.1 fusion.37
  13.1 3.5 %scatter_custom_fusion.1 = bf16[768,896]{1,0:T(8,128)(2,1)S(1)} fusion(s32[512]{0:T(512)S(1)} %bitcast.92, bf16[512,896]{1,0:T(8,128)(2,1)} %reshape.126, bf16[]{:T(256)} %constant.5.clone.1), kind=kCustom, calls=%fused_computation.23 | custom fusion | bytes 1376768 | tf_op jit(solution)/shard_map/scatter | solution.py:31
  16.7 0.0 copy-start.8
  16.7 49.8 %all_to_all.20 = bf16[32,24,896]{2,1,0:T(8,128)(2,1)S(1)} all-to-all(bf16[32,24,896]{2,1,0:T(8,128)(2,1)S(1)} %bitcast.79), channel_id=1, replica_groups=mesh['dp'=8,'expert'=32] {'expert'}, dimensions={0} | all-to-all | bytes 2752512 | tf_op jit(solution)/shard_map/all_to_all | solution.py:37
  66.5 1.1 copy-done.2
  67.6 1.8 fusion.13
  69.4 1.6 copy.25
  71.0 0.0 reduce-scatter.12.cloned.1.call-update
  71.0 0.0 reduce-scatter.14.cloned.1.call-start
  71.1 3.1 fusion.16
  74.2 1.6 copy.27
  75.8 0.0 reduce-scatter.14.cloned.1.call-update
  75.8 0.0 reduce-scatter.10.cloned.1.call-start
  75.9 0.9 copy-done.5
  76.7 1.5 mul.65
  78.2 2.8 mul.66
  81.1 0.1 copy.21
  81.2 0.1 mul.63
  81.3 3.9 %scatter_custom_fusion = bf16[768,896]{1,0:T(8,128)(2,1)S(1)} fusion(s32[512]{0:T(512)S(1)} %bitcast.93, f32[512,896]{1,0:T(8,128)} %mul.66, f32[512]{0:T(512)S(1)} %mul.63, bf16[]{:T(256)} %constant.5.clone.1), kind=kCustom, calls=%fused_computation.21 | custom fusion | flops 917504 | bytes 3213314 | tf_op jit(solution)/shard_map/scatter | solution.py:32
  85.2 0.0 copy-start.7
  85.2 48.7 %all_to_all.21 = bf16[32,24,896]{2,1,0:T(8,128)(2,1)S(1)} all-to-all(bf16[32,24,896]{2,1,0:T(8,128)(2,1)S(1)} %bitcast.78), channel_id=1, replica_groups=mesh['dp'=8,'expert'=32] {'expert'}, dimensions={0} | all-to-all | bytes 2752512 | tf_op jit(solution)/shard_map/all_to_all | solution.py:38
  133.9 1.1 copy-done.4
  135.1 1.8 fusion.10
  136.9 1.6 copy.23
  138.4 0.0 reduce-scatter.10.cloned.1.call-update
  138.5 0.0 all-gather.3.cloned.1.call-start
  138.5 0.0 reduce-scatter.12.cloned.1.call-done
  138.5 1.1 copy.26
  139.6 23.1 %reduce-scatter.14.cloned.1.call-done = bf16[128,768]{1,0:T(8,128)(2,1)} async-done(((bf16[1024,768]{1,0:T(8,128)(2,1)}), bf16[128,768]{1,0:T(8,128)(2,1)}) %reduce-scatter.14.cloned.1.call-update) | async-done | bytes 196624
  162.7 1.1 copy.28
  163.8 44.3 %reduce-scatter.10.cloned.1.call-done = bf16[128,768]{1,0:T(8,128)(2,1)} async-done(((bf16[1024,768]{1,0:T(8,128)(2,1)}), bf16[128,768]{1,0:T(8,128)(2,1)}) %reduce-scatter.10.cloned.1.call-update) | async-done | bytes 196624
  208.1 1.1 copy.24
  209.2 1.0 fusion.29
  210.2 0.0 all-gather.3.cloned.1.call-update
  210.2 0.1 copy.22
  210.4 1.2 stack.2
  211.6 3.8 %all-to-all-start.2 = ((bf16[8,768,128]{1,2,0:T(8,128)(2,1)}), bf16[8,768,128]{1,2,0:T(8,128)(2,1)S(1)}, u32[]{:S(2)}, u32[]{:S(2)}) async-start(bf16[8,768,128]{1,2,0:T(8,128)(2,1)} %stack.2), calls=%async_computation.2 | async-start | bytes 3145728 | tf_op jit(solution)/shard_map/all_to_all | solution.py:64
  215.4 0.0 all-gather.5.cloned.1.call-start
  215.4 0.5 all-gather.5.cloned.1.call-update
  216.0 44.4 %all-gather.3.cloned.1.call-done = bf16[768,1024]{1,0:T(8,128)(2,1)} async-done(((bf16[768,128]{1,0:T(8,128)(2,1)}), bf16[768,1024]{1,0:T(8,128)(2,1)}) %all-gather.3.cloned.1.call-update) | async-done | bytes 1572880 | tf_op jit(solution)/shard_map/all_gather | solution.py:62
  260.4 4.8 %fusion = f32[768,896]{1,0:T(8,128)} fusion(bf16[768,1024]{1,0:T(8,128)(2,1)} %all-gather.3.cloned.1.call-done, bf16[1,896,1024]{2,1,0:T(8,128)(2,1)S(1)} %copy-done), kind=kOutput, calls=%fused_computation.4 | convolution fusion | flops 1409286144 | bytes 6160384 | tf_op jit(solution)/shard_map/dot_general | solution.py:8
  265.2 0.0 all-to-all-done.2
  265.2 5.9 %add_convert_fusion = bf16[768,896]{1,0:T(8,128)(2,1)} fusion(f32[768,896]{1,0:T(8,128)} %fusion, bf16[768,1024]{0,1:T(8,128)(2,1)S(1)} %bitcast.80, bf16[1,896,1024]{2,1,0:T(8,128)(2,1)} %param.12), kind=kOutput, calls=%fused_computation.3 | convolution fusion | flops 1410662400 | bytes 7536640 | tf_op jit(solution)/shard_map/dot_general | solution.py:8
  271.1 13.9 %all-to-all-start.3 = ((bf16[32,24,896]{2,1,0:T(8,128)(2,1)}), bf16[32,24,896]{2,1,0:T(8,128)(2,1)S(1)}, u32[]{:S(2)}, u32[]{:S(2)}) async-start(bf16[32,24,896]{2,1,0:T(8,128)(2,1)} %bitcast.88), calls=%async_computation.3 | async-start | bytes 2752512 | tf_op jit(solution)/shard_map/all_to_all | solution.py:70
  285.0 4.9 %convert_bitcast_fusion.1 = bf16[1,896,1024]{2,1,0:T(8,128)(2,1)} fusion(bf16[768,896]{1,0:T(8,128)(2,1)} %bitcast.84, bf16[768,1024]{0,1:T(8,128)(2,1)} %bitcast.81), kind=kOutput, calls=%fused_computation.15 | convolution fusion | flops 1410203648 | bytes 4784128 | tf_op jit(solution)/shard_map/dot_general | solution.py:8
  290.0 2.9 convert_bitcast_fusion.2
  292.8 32.8 %all-gather.5.cloned.1.call-done = bf16[768,1024]{1,0:T(8,128)(2,1)} async-done(((bf16[768,128]{1,0:T(8,128)(2,1)}), bf16[768,1024]{1,0:T(8,128)(2,1)}) %all-gather.5.cloned.1.call-update) | async-done | bytes 1572880 | tf_op jit(solution)/shard_map/all_gather | solution.py:55
  325.7 4.9 %convert_bitcast_fusion = bf16[1,1024,896]{2,1,0:T(8,128)(2,1)} fusion(bf16[768,1024]{1,0:T(8,128)(2,1)} %all-gather.5.cloned.1.call-done, bf16[768,896]{1,0:T(8,128)(2,1)} %bitcast.87), kind=kOutput, calls=%fused_computation.14 | convolution fusion | flops 1410203648 | bytes 4784128 | tf_op jit(solution)/shard_map/dot_general | solution.py:8
  330.5 2.0 all-to-all-done.3
  332.5 2.7 gather_fusion
  335.2 1.8 reshape.105
  337.0 1.9 reduce_sum.25
  (19 shorter events, 0.1 us)
Async XLA Ops:
  7.2 63.9 %copy-start = (bf16[1,896,1024]{2,1,0:T(8,128)(2,1)S(1)}, bf16[1,896,1024]{2,1,0:T(8,128)(2,1)}, u32[]{:S(2)}) copy-start(bf16[1,896,1024]{2,1,0:T(8,128)(2,1)} %param.11) | copy-start | bytes 5505028
  7.2 131.4 %reduce-scatter.12.cloned.1.call-start = ((), (), s32[]{:S(2)}) async-start(), calls=%async_computation.10 | async-start | bytes 1769472
  16.7 50.9 %copy-start.8 = (bf16[1,896,1024]{2,1,0:T(8,128)(2,1)S(1)}, bf16[1,896,1024]{2,1,0:T(8,128)(2,1)}, u32[]{:S(2)}) copy-start(bf16[1,896,1024]{2,1,0:T(8,128)(2,1)} %param.12) | copy-start | bytes 5505028
  66.5 1.1 copy-start.2
  71.0 91.7 %reduce-scatter.14.cloned.1.call-start = ((), (), s32[]{:S(2)}) async-start(), calls=%async_computation.11 | async-start | bytes 1769472
  75.8 0.9 copy-start.5
  75.8 132.3 %reduce-scatter.10.cloned.1.call-start = ((), (), s32[]{:S(2)}) async-start(), calls=%async_computation.9 | async-start | bytes 1769472
  78.2 2.9 copy-start.6
  85.2 49.8 %copy-start.7 = (bf16[1,1024,896]{2,1,0:T(8,128)(2,1)S(1)}, bf16[1,1024,896]{2,1,0:T(8,128)(2,1)}, u32[]{:S(2)}) copy-start(bf16[1,1024,896]{2,1,0:T(8,128)(2,1)} %param.13) | copy-start | bytes 5505028
  133.9 1.1 copy-start.4
  138.5 121.9 %all-gather.3.cloned.1.call-start = ((), (), s32[]{:S(2)}) async-start(), calls=%async_computation.7 | async-start | bytes 1769472 | tf_op jit(solution)/shard_map/all_gather | solution.py:62
  211.6 53.6 %all-to-all-start.2 = ((bf16[8,768,128]{1,2,0:T(8,128)(2,1)}), bf16[8,768,128]{1,2,0:T(8,128)(2,1)S(1)}, u32[]{:S(2)}, u32[]{:S(2)}) async-start(bf16[8,768,128]{1,2,0:T(8,128)(2,1)} %stack.2), calls=%async_computation.2 | async-start | bytes 3145728 | tf_op jit(solution)/shard_map/all_to_all | solution.py:64
  215.4 110.3 %all-gather.5.cloned.1.call-start = ((), (), s32[]{:S(2)}) async-start(), calls=%async_computation.8 | async-start | bytes 1769472 | tf_op jit(solution)/shard_map/all_gather | solution.py:55
  265.2 5.9 %copy-start.1 = (bf16[8,768,128]{1,2,0:T(8,128)(2,1)}, bf16[8,768,128]{1,2,0:T(8,128)(2,1)S(1)}, u32[]{:S(2)}) copy-start(bf16[8,768,128]{1,2,0:T(8,128)(2,1)S(1)} %all-to-all-done.2) | copy-start | bytes 4718596
  271.1 61.4 %all-to-all-start.3 = ((bf16[32,24,896]{2,1,0:T(8,128)(2,1)}), bf16[32,24,896]{2,1,0:T(8,128)(2,1)S(1)}, u32[]{:S(2)}, u32[]{:S(2)}) async-start(bf16[32,24,896]{2,1,0:T(8,128)(2,1)} %bitcast.88), calls=%async_computation.3 | async-start | bytes 2752512 | tf_op jit(solution)/shard_map/all_to_all | solution.py:70
  285.0 4.9 %copy-start.3 = (bf16[32,24,896]{2,1,0:T(8,128)(2,1)S(1)}, bf16[32,24,896]{2,1,0:T(8,128)(2,1)}, u32[]{:S(2)}) copy-start(bf16[32,24,896]{2,1,0:T(8,128)(2,1)} %copy-done.2) | copy-start | bytes 4128772
  285.0 4.9 %copy-start.9 = (bf16[768,1024]{1,0:T(8,128)(2,1)S(1)}, bf16[768,1024]{1,0:T(8,128)(2,1)}, u32[]{:S(2)}) copy-start(bf16[768,1024]{1,0:T(8,128)(2,1)} %all-gather.3.cloned.1.call-done) | copy-start | bytes 4718596
Sparse Core Ops, SparseCore 0:
  71.1 49.0 reduce-scatter.11
  122.7 39.9 reduce-scatter.13
  165.9 42.1 reduce-scatter.9
  210.3 49.9 all-gather.2
  262.5 63.1 all-gather.4
